TPU v7x, 32 devices: a whole 2x2x4 slice. The times are simulated.
32 devices in a mesh: rep: 8 (over z, y), grp: 4 (over x, core).
Axes of the slice: x: 2, y: 2, z: 4, core: 2. Of those that a mesh axis runs over, the one named last changes fastest.
Arguments:
- tokens: bfloat16 [3648, 1152], P(('rep', 'grp')), may hold values from -6 to 6
- cotangent: bfloat16 [3648, 1152], P(('rep', 'grp')), may hold values from -6 to 6
- slice_sizes: int32 [32], replicated, may hold values from 113 to 114, as said below
- gain_one: float32 [1152], replicated, may hold values from 0.1 to 1.9
- shift_one: float32 [1152], replicated, may hold values from -3 to 3
- attn_in: bfloat16 [3456, 1152], P('grp')
- attn_bias: float32 [2, 1152], replicated, may hold values from -3 to 3
- attn_out: bfloat16 [1152, 1152], P('grp'), may hold values from -1 to 1
- out_bias: float32 [1152], replicated, may hold values from -3 to 3
- gain_two: float32 [1152], replicated, may hold values from 0.1 to 1.9
- shift_two: float32 [1152], replicated, may hold values from -3 to 3
- mlp_up: bfloat16 [4304, 1152], P('grp'), may hold values from -0.1875 to 0.1875
- up_bias: float32 [4304], replicated, may hold values from -3 to 3
- mlp_down: bfloat16 [4304, 1152], P('grp'), may hold values from -0.09375 to 0.09375
- down_bias: float32 [1152], replicated, may hold values from -3 to 3
Outputs:
- block_output: bfloat16 [3648, 1152], P(('rep', 'grp'))
- input_grad: float32 [3648, 1152], P(('rep', 'grp'))
- dgain_one: float32 [1152], replicated
- dshift_one: float32 [1152], replicated
- dattn_in: float32 [3456, 1152], P('grp', 'rep')
- dattn_bias: float32 [2, 1152], replicated
- dattn_out: float32 [1152, 1152], P('grp', 'rep')
- dout_bias: float32 [1152], replicated
- dgain_two: float32 [1152], replicated
- dshift_two: float32 [1152], replicated
- dmlp_up: float32 [4304, 1152], P('grp', 'rep')
- dup_bias: float32 [4304], replicated
- dmlp_down: float32 [4304, 1152], P('grp', 'rep')
- ddown_bias: float32 [1152], replicated
Inputs may be any that keep to these rules, and one draw needn't show every extreme that they name: slice_sizes sums to 3645; every entry is 113 or one more.
All inputs are finite; a program needn't handle non-finite values.
Results may differ from a plain program's by a relative error of at most 0.012.
Values may be sent and summed in bfloat16 or wider, within the bound.
A program may use at most 192 MiB of HBM per device.

v0:
```python
import jax
import jax.numpy as jnp
from jax import lax
from jax.sharding import PartitionSpec as P

H = 16
HD = 72
IMG = 729


EPSILON = 1e-06
SQRT_TWO_PI = 0.7978845608028654
CUBIC = 0.044715
NEGATIVE = -1e30


def passed_along(block, axis, distance):
    devices = range(lax.axis_size(axis))
    route = [(i - distance, i) for i in devices if i - distance in devices]
    return lax.ppermute(block, axis, route)


def norm_forward(rows, gain_row, shift_row):
    centered = rows - jnp.mean(rows, axis=-1, keepdims=True)
    inverse = lax.rsqrt(jnp.mean(centered * centered, axis=-1, keepdims=True) + EPSILON)
    normed = centered * inverse
    return (normed, inverse, normed * gain_row + shift_row)


def norm_backward(dscaled, normed, inverse, gain_row):
    dnormed = dscaled * gain_row
    return inverse * (
        dnormed
        - jnp.mean(dnormed, axis=-1, keepdims=True)
        - normed * jnp.mean(dnormed * normed, axis=-1, keepdims=True)
    )


def gelu_parts(before):
    inside = SQRT_TWO_PI * (before + CUBIC * before * before * before)
    tangent = jnp.tanh(inside)
    activated = 0.5 * before * (1.0 + tangent)
    derivative = 0.5 * (1.0 + tangent) + 0.5 * before * (1.0 - tangent * tangent) * SQRT_TWO_PI * (
        1.0 + 3.0 * CUBIC * before * before
    )
    return (activated, derivative)


def owned_grads(left_one, right_one, left_two, right_two):
    all_left_one, all_right_one, all_left_two, all_right_two = (
        lax.all_gather(left_one, "grp", axis=0, tiled=True),
        lax.all_gather(right_one, "grp", axis=0, tiled=True),
        lax.all_gather(left_two, "grp", axis=0, tiled=True),
        lax.all_gather(right_two, "grp", axis=0, tiled=True),
    )
    member = lax.axis_index("grp")
    groups = lax.axis_size("grp")
    rows_one = left_one.shape[1] // groups
    rows_two = left_two.shape[1] // groups
    picked_one = lax.dynamic_slice_in_dim(all_left_one, member * rows_one, rows_one, 1)
    picked_two = lax.dynamic_slice_in_dim(all_left_two, member * rows_two, rows_two, 1)
    grad_one = jnp.dot(picked_one.T, all_right_one, preferred_element_type=jnp.float32)
    grad_two = jnp.dot(picked_two.T, all_right_two, preferred_element_type=jnp.float32)
    return (grad_one, grad_two)


def replica_sums(first_rows, second_rows):
    return (
        lax.psum_scatter(first_rows, "rep", scatter_dimension=1, tiled=True),
        lax.psum_scatter(second_rows, "rep", scatter_dimension=1, tiled=True),
    )


def per_device(
    tokens,
    cotangent,
    slice_sizes,
    gain_one,
    shift_one,
    attn_in,
    attn_bias,
    attn_out,
    out_bias,
    gain_two,
    shift_two,
    mlp_up,
    up_bias,
    mlp_down,
    down_bias,
):
    capacity, width = tokens.shape
    base_rows = capacity - 1
    reach = (IMG - 2 + base_rows) // base_rows
    windows = (capacity + IMG - 2) // IMG + 1
    window_keys = windows * IMG
    score_scale = HD ** (-0.5)
    device = lax.axis_index(("rep", "grp"))
    starts = jnp.cumsum(slice_sizes) - slice_sizes
    own_start = starts[device]
    own_count = slice_sizes[device]
    row_index = jnp.arange(capacity, dtype=jnp.int32)
    is_live = row_index < own_count
    live_col = is_live[:, None]
    query_image = (own_start + row_index) // IMG
    first_image = own_start // IMG
    last_image = (own_start + own_count - 1) // IMG
    window_image = first_image + jnp.arange(windows, dtype=jnp.int32)
    key_image = jnp.repeat(jnp.minimum(window_image, last_image), IMG)
    key_live = jnp.repeat(window_image <= last_image, IMG)
    key_place = key_image * IMG + jnp.tile(jnp.arange(IMG, dtype=jnp.int32), windows)
    earlier = starts[None, :] <= key_place[:, None]
    owner = jnp.sum(earlier.astype(jnp.int32), axis=1) - 1
    owner_start = jnp.max(jnp.where(earlier, starts[None, :], 0), axis=1)
    buffer_row = (owner - device + reach) * capacity + key_place - owner_start
    allowed = (query_image[:, None] == key_image[None, :]) & key_live[None, :] & live_col
    full_in, full_out, full_up, full_down = (
        lax.all_gather(attn_in, "grp", axis=0, tiled=True),
        lax.all_gather(attn_out, "grp", axis=0, tiled=True),
        lax.all_gather(mlp_up, "grp", axis=0, tiled=True),
        lax.all_gather(mlp_down, "grp", axis=0, tiled=True),
    )
    tokens_f = tokens.astype(jnp.float32)
    normed_one, inverse_one, scaled_one = norm_forward(tokens_f, gain_one, shift_one)
    first = scaled_one.astype(jnp.bfloat16)
    bias_full = jnp.concatenate([attn_bias[0], jnp.zeros((width,), jnp.float32), attn_bias[1]])
    projected = jnp.dot(first, full_in.T, preferred_element_type=jnp.float32) + bias_full
    queries = projected[:, :width].astype(jnp.bfloat16)
    keyvalue = projected[:, width:].astype(jnp.bfloat16)
    pieces = []
    for offset in range(-reach, reach + 1):
        if offset == 0:
            pieces.append(keyvalue)
        else:
            pieces.append(passed_along(keyvalue, ("rep", "grp"), -offset))
    neighbours = jnp.concatenate(pieces, axis=0)
    window = neighbours[buffer_row]
    keys3 = window[:, :width].reshape(window_keys, H, HD)
    values3 = window[:, width:].reshape(window_keys, H, HD)
    queries3 = queries.reshape(capacity, H, HD)

    def masked_scores():
        raw = (
            jnp.einsum("qhd,khd->hqk", queries3, keys3, preferred_element_type=jnp.float32)
            * score_scale
        )
        return jnp.where(allowed[None], raw, NEGATIVE)

    scores = masked_scores()
    highest = jnp.max(scores, axis=-1, keepdims=True)
    logsum = highest + jnp.log(jnp.sum(jnp.exp(scores - highest), axis=-1, keepdims=True))
    weights = jnp.where(allowed[None], jnp.exp(scores - logsum), 0.0).astype(jnp.bfloat16)
    mixed = (
        jnp.einsum("hqk,khd->qhd", weights, values3, preferred_element_type=jnp.float32)
        .astype(jnp.bfloat16)
        .reshape(capacity, width)
    )
    resid = tokens_f + jnp.dot(mixed, full_out, preferred_element_type=jnp.float32) + out_bias
    normed_two, inverse_two, scaled_two = norm_forward(resid, gain_two, shift_two)
    second = scaled_two.astype(jnp.bfloat16)
    before = jnp.dot(second, full_up.T, preferred_element_type=jnp.float32) + up_bias
    activated, derivative = gelu_parts(before)
    hidden = activated.astype(jnp.bfloat16)
    final = resid + jnp.dot(hidden, full_down, preferred_element_type=jnp.float32) + down_bias
    block_output = jnp.where(live_col, final, 0.0).astype(jnp.bfloat16)
    dfinal_b = jnp.where(live_col, cotangent, jnp.zeros_like(cotangent))
    dfinal = dfinal_b.astype(jnp.float32)
    dbefore = jnp.dot(dfinal_b, full_down.T, preferred_element_type=jnp.float32) * derivative
    dbefore_b = dbefore.astype(jnp.bfloat16)
    dsecond = jnp.dot(dbefore_b, full_up, preferred_element_type=jnp.float32)
    dresid = dfinal + norm_backward(dsecond, normed_two, inverse_two, gain_two)
    mlp_up_rows, mlp_down_rows = owned_grads(dbefore_b, second, hidden, dfinal_b)
    dmlp_up, dmlp_down = replica_sums(mlp_up_rows, mlp_down_rows)
    dresid_b = dresid.astype(jnp.bfloat16)
    dmixed = jnp.dot(dresid_b, full_out.T, preferred_element_type=jnp.float32).astype(jnp.bfloat16)
    dmixed3 = dmixed.reshape(capacity, H, HD)
    delta = jnp.sum(
        dmixed3.astype(jnp.float32) * mixed.reshape(capacity, H, HD).astype(jnp.float32), axis=-1
    ).T
    scores = masked_scores()
    probs = jnp.where(allowed[None], jnp.exp(scores - logsum), 0.0)
    dprob = jnp.einsum("qhd,khd->hqk", dmixed3, values3, preferred_element_type=jnp.float32)
    dscore = (probs * (dprob - delta[:, :, None]) * score_scale).astype(jnp.bfloat16)
    dquery = jnp.einsum("hqk,khd->qhd", dscore, keys3, preferred_element_type=jnp.float32).reshape(
        capacity, width
    )
    dkey = jnp.einsum("hqk,qhd->khd", dscore, queries3, preferred_element_type=jnp.float32).reshape(
        window_keys, width
    )
    dvalue = jnp.einsum(
        "hqk,qhd->khd", weights, dmixed3, preferred_element_type=jnp.float32
    ).reshape(window_keys, width)
    dwindow = jnp.concatenate([dkey, dvalue], axis=1)
    dneighbours = (
        jnp.zeros((neighbours.shape[0], 2 * width), jnp.float32).at[buffer_row].add(dwindow)
    )
    dkeyvalue = dneighbours[reach * capacity : (reach + 1) * capacity]
    for offset in range(-reach, reach + 1):
        if offset != 0:
            segment = dneighbours[(offset + reach) * capacity : (offset + reach + 1) * capacity]
            dkeyvalue = dkeyvalue + passed_along(segment, ("rep", "grp"), offset)
    dprojected = jnp.concatenate([dquery, dkeyvalue], axis=1).astype(jnp.bfloat16)
    attn_in_rows, attn_out_rows = owned_grads(dprojected, first, mixed, dresid_b)
    dattn_in, dattn_out = replica_sums(attn_in_rows, attn_out_rows)
    dfirst = jnp.dot(dprojected, full_in, preferred_element_type=jnp.float32)
    input_grad = jnp.where(
        live_col, dresid + norm_backward(dfirst, normed_one, inverse_one, gain_one), 0.0
    )
    dgain_one, dshift_one, dattn_bias, dout_bias, dgain_two, dshift_two, dup_bias, ddown_bias = (
        lax.psum(
            (
                jnp.sum(dfirst * normed_one, axis=0),
                jnp.sum(dfirst, axis=0),
                jnp.stack([jnp.sum(dquery, axis=0), jnp.sum(dkeyvalue[:, width:], axis=0)]),
                jnp.sum(dresid, axis=0),
                jnp.sum(dsecond * normed_two, axis=0),
                jnp.sum(dsecond, axis=0),
                jnp.sum(dbefore, axis=0),
                jnp.sum(dfinal, axis=0),
            ),
            ("rep", "grp"),
        )
    )
    return (
        block_output,
        input_grad,
        dgain_one,
        dshift_one,
        dattn_in,
        dattn_bias,
        dattn_out,
        dout_bias,
        dgain_two,
        dshift_two,
        dmlp_up,
        dup_bias,
        dmlp_down,
        ddown_bias,
    )


def solution(mesh):
    in_specs = (
        P(("rep", "grp"), None),
        P(("rep", "grp"), None),
        P(),
        P(),
        P(),
        P("grp", None),
        P(),
        P("grp", None),
        P(),
        P(),
        P(),
        P("grp", None),
        P(),
        P("grp", None),
        P(),
    )
    out_specs = (
        P(("rep", "grp"), None),
        P(("rep", "grp"), None),
        P(),
        P(),
        P("grp", "rep"),
        P(),
        P("grp", "rep"),
        P(),
        P(),
        P(),
        P("grp", "rep"),
        P(),
        P("grp", "rep"),
        P(),
    )
    return jax.shard_map(
        per_device, mesh=mesh, in_specs=in_specs, out_specs=out_specs, check_vma=False
    )
```

profile of v0, /device:TPU:0, one launch (start us, length us, event | category | flops | bytes accessed | tf_op | source)
XLA Modules:
  0.0 1322.6 jit_solution(18031253088932466341)
XLA Ops:
  15.5 52.6 %all-gather.23.cloned.1.call-done = bf16[3456,1152]{1,0:T(8,128)(2,1)} async-done(((bf16[864,1152]{1,0:T(8,128)(2,1)}), bf16[3456,1152]{1,0:T(8,128)(2,1)}) %all-gather.23.cloned.1.call-update) | async-done | bytes 7962640 | tf_op jit(solution)/shard_map/all_gather | solution.py:117
  68.2 6.1 fusion.7
  81.3 20.4 %collective-permute-done.13 = bf16[114,2304]{1,0:T(8,128)(2,1)S(1)} collective-permute-done((bf16[114,2304]{1,0:T(8,128)(2,1)S(1)}, bf16[114,2304]{1,0:T(8,128)(2,1)S(1)}, u32[]{:S(2)}, u32[]{:S(2)}) %collective-permute-start.13) | collective-permute-done | bytes 525344 | tf_op jit(solution)/shard_map/ppermute | solution.py:20
  107.0 13.9 %collective-permute-start.6 = (bf16[114,2304]{1,0:T(8,128)(2,1)S(1)}, bf16[114,2304]{1,0:T(8,128)(2,1)S(1)}, u32[]{:S(2)}, u32[]{:S(2)}) collective-permute-start(bf16[114,2304]{1,0:T(8,128)(2,1)S(1)} %slice.92), channel_id=1, source_target_pairs={{0,1},{1,2},{2,3},{3,4},{4,5},{5,6},{6,7},{7,8},{8,9},{9,10},{10,1... | collective-permute-start | bytes 1575944 | tf_op jit(solution)/shard_map/ppermute | solution.py:20
  120.8 3.5 collective-permute-start.5
  125.1 3.0 collective-permute-done.9
  128.2 5.9 collective-permute-start.4
  134.1 17.2 %collective-permute-start.3 = (bf16[114,2304]{1,0:T(8,128)(2,1)S(1)}, bf16[114,2304]{1,0:T(8,128)(2,1)}, u32[]{:S(2)}, u32[]{:S(2)}) collective-permute-start(bf16[114,2304]{1,0:T(8,128)(2,1)S(1)} %slice.92), channel_id=1, source_target_pairs={{0,4},{1,5},{2,6},{3,7},{4,8},{5,9},{6,10},{7,11},{8,12},{9,13},{1... | collective-permute-start | bytes 1575944 | tf_op jit(solution)/shard_map/ppermute | solution.py:20
  151.3 3.8 collective-permute-start.2
  155.1 28.5 %collective-permute-start.1 = (bf16[114,2304]{1,0:T(8,128)(2,1)S(1)}, bf16[114,2304]{1,0:T(8,128)(2,1)}, u32[]{:S(2)}, u32[]{:S(2)}) collective-permute-start(bf16[114,2304]{1,0:T(8,128)(2,1)S(1)} %slice.92), channel_id=1, source_target_pairs={{0,6},{1,7},{2,8},{3,9},{4,10},{5,11},{6,12},{7,13},{8,14},{9,15},... | collective-permute-start | bytes 1575944 | tf_op jit(solution)/shard_map/ppermute | solution.py:20
  183.6 8.0 collective-permute-start
  194.2 19.5 %collective-permute-done.1 = bf16[114,2304]{1,0:T(8,128)(2,1)} collective-permute-done((bf16[114,2304]{1,0:T(8,128)(2,1)S(1)}, bf16[114,2304]{1,0:T(8,128)(2,1)}, u32[]{:S(2)}, u32[]{:S(2)}) %collective-permute-start.1) | collective-permute-done | bytes 525344 | tf_op jit(solution)/shard_map/ppermute | solution.py:20
  213.7 21.3 %collective-permute-done = bf16[114,2304]{1,0:T(8,128)(2,1)} collective-permute-done((bf16[114,2304]{1,0:T(8,128)(2,1)S(1)}, bf16[114,2304]{1,0:T(8,128)(2,1)}, u32[]{:S(2)}, u32[]{:S(2)}) %collective-permute-start) | collective-permute-done | bytes 525344 | tf_op jit(solution)/shard_map/ppermute | solution.py:20
  235.0 57.9 %concatenate.14 = bf16[1710,2304]{1,0:T(8,128)(2,1)} concatenate(bf16[114,2304]{1,0:T(8,128)(2,1)} %collective-permute-done, bf16[114,2304]{1,0:T(8,128)(2,1)} %collective-permute-done.1, bf16[114,2304]{1,0:T(8,128)(2,1)} %collective-permute-done.2, bf16[114,2304]{1,0:T(8,128)(2,1)} %collective-permute-done.3, bf16[114,2304]{1,0:T(8,128)(2,1)} %collective-permute-done.4, ...), dimensions={0} | concatenate | bytes 15759360 | tf_op jit(solution)/shard_map/concatenate | solution.py:135
  292.9 18.3 %gather_fusion = bf16[1458,2304]{1,0:T(8,128)(2,1)} fusion(bf16[1710,2304]{1,0:T(8,128)(2,1)} %concatenate.14, s32[2048]{0:T(1024)S(1)} %pad_clamp_fusion), kind=kCustom, calls=%fused_computation | custom fusion | bytes 13442760 | tf_op jit(solution)/shard_map/gather | solution.py:136
  311.2 6.4 fusion.80
  317.6 4.4 copy.57
  322.0 6.3 copy.55
  328.2 3.6 fusion.6
  331.9 2.9 exponential_reduce_fusion
  336.3 5.3 convolution_convert_fusion.1
  344.5 11.5 reshape.322
  356.0 7.4 convolution_add_fusion
  363.5 12.1 reshape.324
  375.5 6.3 convolution_multiply_fusion
  381.9 6.2 fusion.53
  396.6 11.5 fusion.73
  408.1 7.2 multiply_convert_fusion
  415.3 8.0 copy.60
  423.3 6.6 fusion.84
  429.9 7.9 copy.59
  437.8 29.8 %scatter_custom_fusion = f32[1710,2304]{1,0:T(8,128)} fusion(s32[1458]{0:T(1024)} %copy-done.35, f32[1458,1152]{1,0:T(8,128)} %copy.60, f32[]{:T(128)} %constant.83.clone.1, f32[1458,1152]{1,0:T(8,128)} %copy.59, f32[]{:T(128)} %constant.37.clone.1), kind=kCustom, calls=%fused_computation.2 | custom fusion | flops 6718464 | bytes 29252608 | tf_op jit(solution)/shard_map/scatter-add | solution.py:194
  467.6 10.2 fusion.79
  479.2 5.7 collective-permute-start.27
  487.6 7.4 collective-permute-start.24
  498.2 13.1 collective-permute-done.27
  513.5 21.4 %collective-permute-done.26 = f32[114,2304]{1,0:T(8,128)S(1)} collective-permute-done((f32[114,2304]{1,0:T(8,128)S(1)}, f32[114,2304]{1,0:T(8,128)S(1)}, u32[]{:S(2)}, u32[]{:S(2)}) %collective-permute-start.26) | collective-permute-done | bytes 1050656 | tf_op jit(solution)/shard_map/ppermute | solution.py:20
  537.3 15.8 %collective-permute-done.25 = f32[114,2304]{1,0:T(8,128)S(1)} collective-permute-done((f32[114,2304]{1,0:T(8,128)S(1)}, f32[114,2304]{1,0:T(8,128)S(1)}, u32[]{:S(2)}, u32[]{:S(2)}) %collective-permute-start.25) | collective-permute-done | bytes 1050656 | tf_op jit(solution)/shard_map/ppermute | solution.py:20
  556.3 20.5 %collective-permute-done.24 = f32[114,2304]{1,0:T(8,128)} collective-permute-done((f32[114,2304]{1,0:T(8,128)}, f32[114,2304]{1,0:T(8,128)}, u32[]{:S(2)}, u32[]{:S(2)}) %collective-permute-start.24) | collective-permute-done | bytes 1050656 | tf_op jit(solution)/shard_map/ppermute | solution.py:20
  579.5 32.6 %collective-permute-done.22 = f32[114,2304]{1,0:T(8,128)} collective-permute-done((f32[114,2304]{1,0:T(8,128)}, f32[114,2304]{1,0:T(8,128)}, u32[]{:S(2)}, u32[]{:S(2)}) %collective-permute-start.22) | collective-permute-done | bytes 1050656 | tf_op jit(solution)/shard_map/ppermute | solution.py:20
  616.4 6.1 fusion.81
  623.9 10.4 collective-permute-done.19
  634.7 61.3 %collective-permute-done.17 = f32[114,2304]{1,0:T(8,128)} collective-permute-done((f32[114,2304]{1,0:T(8,128)}, f32[114,2304]{1,0:T(8,128)}, u32[]{:S(2)}, u32[]{:S(2)}) %collective-permute-start.17) | collective-permute-done | bytes 1050656 | tf_op jit(solution)/shard_map/ppermute | solution.py:20
  697.4 7.7 fusion.76
  705.1 4.8 fusion.49
  713.3 3.4 fusion.72
  724.1 72.8 %all-gather.33.cloned.1.call-done = bf16[4,114,1152]{2,1,0:T(8,128)(2,1)} async-done(((bf16[1,114,1152]{2,1,0:T(8,128)(2,1)}), bf16[4,114,1152]{2,1,0:T(8,128)(2,1)}) %all-gather.33.cloned.1.call-update) | async-done | bytes 1050640 | tf_op jit(solution)/shard_map/all_gather | solution.py:52
  799.4 28.5 %all-gather.31.cloned.1.call-done = bf16[4,114,3456]{2,1,0:T(8,128)(2,1)} async-done(((bf16[1,114,3456]{2,1,0:T(8,128)(2,1)}), bf16[4,114,3456]{2,1,0:T(8,128)(2,1)}) %all-gather.31.cloned.1.call-update) | async-done | bytes 3151888 | tf_op jit(solution)/shard_map/all_gather | solution.py:51
  827.9 2.8 reshape.326
  830.7 4.8 fusion.34
  835.7 11.4 all-gather.45.cloned.1.call-done
  848.6 34.3 %all-gather.43.cloned.1.call-done = bf16[4,114,4304]{2,1,0:T(8,128)(2,1)} async-done(((bf16[1,114,4304]{2,1,0:T(8,128)(2,1)}), bf16[4,114,4304]{2,1,0:T(8,128)(2,1)}) %all-gather.43.cloned.1.call-update) | async-done | bytes 3925264 | tf_op jit(solution)/shard_map/all_gather | solution.py:53
  882.9 6.0 reshape.338
  888.9 5.4 fusion.30
  894.4 7.7 all-gather.41.cloned.1.call-done
  903.6 34.3 %all-gather.39.cloned.1.call-done = bf16[4,114,4304]{2,1,0:T(8,128)(2,1)} async-done(((bf16[1,114,4304]{2,1,0:T(8,128)(2,1)}), bf16[4,114,4304]{2,1,0:T(8,128)(2,1)}) %all-gather.39.cloned.1.call-update) | async-done | bytes 3925264 | tf_op jit(solution)/shard_map/all_gather | solution.py:51
  937.9 6.0 reshape.334
  943.9 5.4 fusion.32
  951.1 6.5 fusion.11
  957.7 42.1 %all-reduce = (f32[1152]{0:T(1024)}, f32[1152]{0:T(1024)}, f32[2,1152]{1,0:T(2,128)}, f32[1152]{0:T(1024)}, f32[1152]{0:T(1024)}, /*index=5*/f32[1152]{0:T(1024)}, f32[4304]{0:T(1024)}, f32[1152]{0:T(1024)}) all-reduce(f32[1152]{0:T(1024)S(1)} %get-tuple-element.16, ...), channel_id=1, replica_groups=mesh['rep'=8,'grp'=4] {'rep','grp'}, use_global_device_ids=true, to_apply=%region_16.17 | all-reduce | flops 13520 | bytes 108160 | tf_op jit(solution)/shard_map/psum | solution.py:209
  999.8 8.9 reduce-scatter.7.cloned.1.call-done
  1008.7 90.7 %reduce-scatter.5.cloned.1.call-done = f32[864,144]{0,1:T(8,128)} async-done(((f32[864,1152]{0,1:T(8,128)}), f32[864,144]{0,1:T(8,128)}) %reduce-scatter.5.cloned.1.call-update) | async-done | bytes 497680 | tf_op jit(solution)/shard_map/reduce_scatter | solution.py:69
  1099.5 108.2 %reduce-scatter.11.cloned.1.call-done = f32[1076,144]{0,1:T(8,128)} async-done(((f32[1076,1152]{0,1:T(8,128)}), f32[1076,144]{0,1:T(8,128)}) %reduce-scatter.11.cloned.1.call-update) | async-done | bytes 619792 | tf_op jit(solution)/shard_map/reduce_scatter | solution.py:70
  1207.7 108.2 %reduce-scatter.9.cloned.1.call-done = f32[1076,144]{0,1:T(8,128)} async-done(((f32[1076,1152]{0,1:T(8,128)}), f32[1076,144]{0,1:T(8,128)}) %reduce-scatter.9.cloned.1.call-update) | async-done | bytes 619792 | tf_op jit(solution)/shard_map/reduce_scatter | solution.py:69
  (251 shorter events, 76.2 us)
Async XLA Ops:
  7.2 61.0 %all-gather.23.cloned.1.call-start = ((), (), s32[]{:S(2)}) async-start(), calls=%async_computation.4 | async-start | bytes 9953280 | tf_op jit(solution)/shard_map/all_gather | solution.py:117
  7.9 333.7 %all-gather.25.cloned.1.call-start = ((), (), s32[]{:S(2)}) async-start(), calls=%async_computation.5 | async-start | bytes 3317760 | tf_op jit(solution)/shard_map/all_gather | solution.py:118
  8.7 335.8 %all-gather.27.cloned.1.call-start = ((), (), s32[]{:S(2)}) async-start(), calls=%async_computation.10 | async-start | bytes 12441600 | tf_op jit(solution)/shard_map/all_gather | solution.py:119
  9.4 58.8 %copy-start.37 = (f32[1152]{0:T(1024)S(1)}, f32[1152]{0:T(1024)}, u32[]{:S(2)}) copy-start(f32[1152]{0:T(1024)} %param.19) | copy-start | bytes 13828
  9.4 58.7 %copy-start.39 = (f32[1152]{0:T(1024)S(1)}, f32[1152]{0:T(1024)}, u32[]{:S(2)}) copy-start(f32[1152]{0:T(1024)} %param.18) | copy-start | bytes 13828
  9.4 354.0 %all-gather.29.cloned.1.call-start = ((), (), s32[]{:S(2)}) async-start(), calls=%async_computation.11 | async-start | bytes 12441600 | tf_op jit(solution)/shard_map/all_gather | solution.py:120
  10.0 708.7 %all-gather.35.cloned.1.call-start = ((), (), s32[]{:S(2)}) async-start(), calls=%async_computation.14 | async-start | bytes 1382400 | tf_op jit(solution)/shard_map/all_gather | solution.py:53
  15.2 52.9 %copy-start.48 = (f32[114]{0:T(128)}, f32[114]{0:T(128)S(1)}, u32[]{:S(2)}) copy-start(f32[114]{0:T(128)S(1)} %broadcast_multiply_fusion.6) | copy-start | bytes 1372
  15.5 52.7 %copy-start.50 = (f32[114]{0:T(128)}, f32[114]{0:T(128)S(1)}, u32[]{:S(2)}) copy-start(f32[114]{0:T(128)S(1)} %add_rsqrt_fusion.1) | copy-start | bytes 1372
  74.3 27.4 %collective-permute-start.13 = (bf16[114,2304]{1,0:T(8,128)(2,1)S(1)}, bf16[114,2304]{1,0:T(8,128)(2,1)S(1)}, u32[]{:S(2)}, u32[]{:S(2)}) collective-permute-start(bf16[114,2304]{1,0:T(8,128)(2,1)S(1)} %slice.92), channel_id=1, source_target_pairs={{7,0},{8,1},{9,2},{10,3},{11,4},{12,5},{13,6},{14,7},{15,8},{16,9}... | collective-permute-start | bytes 1575944 | tf_op jit(solution)/shard_map/ppermute | solution.py:20
  75.6 30.0 %collective-permute-start.12 = (bf16[114,2304]{1,0:T(8,128)(2,1)S(1)}, bf16[114,2304]{1,0:T(8,128)(2,1)S(1)}, u32[]{:S(2)}, u32[]{:S(2)}) collective-permute-start(bf16[114,2304]{1,0:T(8,128)(2,1)S(1)} %slice.92), channel_id=1, source_target_pairs={{6,0},{7,1},{8,2},{9,3},{10,4},{11,5},{12,6},{13,7},{14,8},{15,9},... | collective-permute-start | bytes 1575944 | tf_op jit(solution)/shard_map/ppermute | solution.py:20
  76.9 30.0 %collective-permute-start.11 = (bf16[114,2304]{1,0:T(8,128)(2,1)S(1)}, bf16[114,2304]{1,0:T(8,128)(2,1)S(1)}, u32[]{:S(2)}, u32[]{:S(2)}) collective-permute-start(bf16[114,2304]{1,0:T(8,128)(2,1)S(1)} %slice.92), channel_id=1, source_target_pairs={{5,0},{6,1},{7,2},{8,3},{9,4},{10,5},{11,6},{12,7},{13,8},{14,9},{... | collective-permute-start | bytes 1575944 | tf_op jit(solution)/shard_map/ppermute | solution.py:20
  78.2 42.6 %collective-permute-start.10 = (bf16[114,2304]{1,0:T(8,128)(2,1)S(1)}, bf16[114,2304]{1,0:T(8,128)(2,1)}, u32[]{:S(2)}, u32[]{:S(2)}) collective-permute-start(bf16[114,2304]{1,0:T(8,128)(2,1)S(1)} %slice.92), channel_id=1, source_target_pairs={{4,0},{5,1},{6,2},{7,3},{8,4},{9,5},{10,6},{11,7},{12,8},{13,9},{1... | collective-permute-start | bytes 1575944 | tf_op jit(solution)/shard_map/ppermute | solution.py:20
  80.0 48.1 %collective-permute-start.9 = (bf16[114,2304]{1,0:T(8,128)(2,1)S(1)}, bf16[114,2304]{1,0:T(8,128)(2,1)S(1)}, u32[]{:S(2)}, u32[]{:S(2)}) collective-permute-start(bf16[114,2304]{1,0:T(8,128)(2,1)S(1)} %slice.92), channel_id=1, source_target_pairs={{3,0},{4,1},{5,2},{6,3},{7,4},{8,5},{9,6},{10,7},{11,8},{12,9},{13... | collective-permute-start | bytes 1575944 | tf_op jit(solution)/shard_map/ppermute | solution.py:20
  101.7 32.4 %collective-permute-start.8 = (bf16[114,2304]{1,0:T(8,128)(2,1)S(1)}, bf16[114,2304]{1,0:T(8,128)(2,1)S(1)}, u32[]{:S(2)}, u32[]{:S(2)}) collective-permute-start(bf16[114,2304]{1,0:T(8,128)(2,1)S(1)} %slice.92), channel_id=1, source_target_pairs={{2,0},{3,1},{4,2},{5,3},{6,4},{7,5},{8,6},{9,7},{10,8},{11,9},{12,... | collective-permute-start | bytes 1575944 | tf_op jit(solution)/shard_map/ppermute | solution.py:20
  105.7 45.6 %collective-permute-start.7 = (bf16[114,2304]{1,0:T(8,128)(2,1)S(1)}, bf16[114,2304]{1,0:T(8,128)(2,1)S(1)}, u32[]{:S(2)}, u32[]{:S(2)}) collective-permute-start(bf16[114,2304]{1,0:T(8,128)(2,1)S(1)} %slice.92), channel_id=1, source_target_pairs={{1,0},{2,1},{3,2},{4,3},{5,4},{6,5},{7,6},{8,7},{9,8},{10,9},{11,1... | collective-permute-start | bytes 1575944 | tf_op jit(solution)/shard_map/ppermute | solution.py:20
  107.0 48.2 %collective-permute-start.6 = (bf16[114,2304]{1,0:T(8,128)(2,1)S(1)}, bf16[114,2304]{1,0:T(8,128)(2,1)S(1)}, u32[]{:S(2)}, u32[]{:S(2)}) collective-permute-start(bf16[114,2304]{1,0:T(8,128)(2,1)S(1)} %slice.92), channel_id=1, source_target_pairs={{0,1},{1,2},{2,3},{3,4},{4,5},{5,6},{6,7},{7,8},{8,9},{9,10},{10,1... | collective-permute-start | bytes 1575944 | tf_op jit(solution)/shard_map/ppermute | solution.py:20
  120.8 62.8 %collective-permute-start.5 = (bf16[114,2304]{1,0:T(8,128)(2,1)S(1)}, bf16[114,2304]{1,0:T(8,128)(2,1)S(1)}, u32[]{:S(2)}, u32[]{:S(2)}) collective-permute-start(bf16[114,2304]{1,0:T(8,128)(2,1)S(1)} %slice.92), channel_id=1, source_target_pairs={{0,2},{1,3},{2,4},{3,5},{4,6},{5,7},{6,8},{7,9},{8,10},{9,11},{10,... | collective-permute-start | bytes 1575944 | tf_op jit(solution)/shard_map/ppermute | solution.py:20
  125.0 250.5 %copy-start.45 = (pred[114]{0:T(512)(128)(4,1)}, pred[114]{0:T(512)(128)(4,1)S(1)}, u32[]{:S(2)}) copy-start(pred[114]{0:T(512)(128)(4,1)S(1)} %iota_compare_fusion) | copy-start | bytes 346
  125.1 67.2 %copy-start.35 = (s32[1458]{0:T(1024)}, s32[1458]{0:T(1024)S(1)}, u32[]{:S(2)}) copy-start(s32[1458]{0:T(1024)S(1)} %fusion.60) | copy-start | bytes 17500
  128.2 64.2 %copy-start.28 = (bf16[114,2304]{1,0:T(8,128)(2,1)}, bf16[114,2304]{1,0:T(8,128)(2,1)S(1)}, u32[]{:S(2)}) copy-start(bf16[114,2304]{1,0:T(8,128)(2,1)S(1)} %collective-permute-done.9) | copy-start | bytes 1575940
  128.2 66.0 %collective-permute-start.4 = (bf16[114,2304]{1,0:T(8,128)(2,1)S(1)}, bf16[114,2304]{1,0:T(8,128)(2,1)}, u32[]{:S(2)}, u32[]{:S(2)}) collective-permute-start(bf16[114,2304]{1,0:T(8,128)(2,1)S(1)} %slice.92), channel_id=1, source_target_pairs={{0,3},{1,4},{2,5},{3,6},{4,7},{5,8},{6,9},{7,10},{8,11},{9,12},{10... | collective-permute-start | bytes 1575944 | tf_op jit(solution)/shard_map/ppermute | solution.py:20
  134.1 58.2 %copy-start.29 = (bf16[114,2304]{1,0:T(8,128)(2,1)}, bf16[114,2304]{1,0:T(8,128)(2,1)S(1)}, u32[]{:S(2)}) copy-start(bf16[114,2304]{1,0:T(8,128)(2,1)S(1)} %collective-permute-done.8) | copy-start | bytes 1575940
  134.1 60.1 %collective-permute-start.3 = (bf16[114,2304]{1,0:T(8,128)(2,1)S(1)}, bf16[114,2304]{1,0:T(8,128)(2,1)}, u32[]{:S(2)}, u32[]{:S(2)}) collective-permute-start(bf16[114,2304]{1,0:T(8,128)(2,1)S(1)} %slice.92), channel_id=1, source_target_pairs={{0,4},{1,5},{2,6},{3,7},{4,8},{5,9},{6,10},{7,11},{8,12},{9,13},{1... | collective-permute-start | bytes 1575944 | tf_op jit(solution)/shard_map/ppermute | solution.py:20
  151.3 41.0 %copy-start.30 = (bf16[114,2304]{1,0:T(8,128)(2,1)}, bf16[114,2304]{1,0:T(8,128)(2,1)S(1)}, u32[]{:S(2)}) copy-start(bf16[114,2304]{1,0:T(8,128)(2,1)S(1)} %collective-permute-done.7) | copy-start | bytes 1575940
  151.3 42.9 %collective-permute-start.2 = (bf16[114,2304]{1,0:T(8,128)(2,1)S(1)}, bf16[114,2304]{1,0:T(8,128)(2,1)}, u32[]{:S(2)}, u32[]{:S(2)}) collective-permute-start(bf16[114,2304]{1,0:T(8,128)(2,1)S(1)} %slice.92), channel_id=1, source_target_pairs={{0,5},{1,6},{2,7},{3,8},{4,9},{5,10},{6,11},{7,12},{8,13},{9,14},{... | collective-permute-start | bytes 1575944 | tf_op jit(solution)/shard_map/ppermute | solution.py:20
  155.1 38.1 %copy-start.31 = (bf16[114,2304]{1,0:T(8,128)(2,1)}, bf16[114,2304]{1,0:T(8,128)(2,1)S(1)}, u32[]{:S(2)}) copy-start(bf16[114,2304]{1,0:T(8,128)(2,1)S(1)} %collective-permute-done.6) | copy-start | bytes 1575940
  155.1 58.6 %collective-permute-start.1 = (bf16[114,2304]{1,0:T(8,128)(2,1)S(1)}, bf16[114,2304]{1,0:T(8,128)(2,1)}, u32[]{:S(2)}, u32[]{:S(2)}) collective-permute-start(bf16[114,2304]{1,0:T(8,128)(2,1)S(1)} %slice.92), channel_id=1, source_target_pairs={{0,6},{1,7},{2,8},{3,9},{4,10},{5,11},{6,12},{7,13},{8,14},{9,15},... | collective-permute-start | bytes 1575944 | tf_op jit(solution)/shard_map/ppermute | solution.py:20
  183.6 51.4 %collective-permute-start = (bf16[114,2304]{1,0:T(8,128)(2,1)S(1)}, bf16[114,2304]{1,0:T(8,128)(2,1)}, u32[]{:S(2)}, u32[]{:S(2)}) collective-permute-start(bf16[114,2304]{1,0:T(8,128)(2,1)S(1)} %slice.92), channel_id=1, source_target_pairs={{0,7},{1,8},{2,9},{3,10},{4,11},{5,12},{6,13},{7,14},{8,15},{9,16}... | collective-permute-start | bytes 1575944 | tf_op jit(solution)/shard_map/ppermute | solution.py:20
  344.1 45.2 %copy-start.5 = (f32[114,1152]{1,0:T(8,128)}, f32[114,1152]{1,0:T(8,128)S(1)}, u32[]{:S(2)}) copy-start(f32[114,1152]{1,0:T(8,128)S(1)} %get-tuple-element.68) | copy-start | bytes 1575940
  391.8 16.3 %slice-start = ((s8[11796480]{0:T(1024)(128)(4,1)}), s8[3407872]{0:T(1024)(128)(4,1)S(1)}, s32[]{:S(2)}) async-start(s8[11796480]{0:T(1024)(128)(4,1)} %bitcast.63), calls=%async_computation.20 | async-start | bytes 6815744
  467.6 148.8 %copy-start.2 = (bf16[1458,1152]{0,1:T(8,128)(2,1)S(1)}, bf16[1458,1152]{0,1:T(8,128)(2,1)}, u32[]{:S(2)}) copy-start(bf16[1458,1152]{0,1:T(8,128)(2,1)} %copy-done.1) | copy-start | bytes 10077700
  477.9 18.1 %collective-permute-start.14 = (f32[114,2304]{1,0:T(8,128)S(1)}, f32[114,2304]{1,0:T(8,128)S(1)}, u32[]{:S(2)}, u32[]{:S(2)}) collective-permute-start(f32[114,2304]{1,0:T(8,128)S(1)} %get-tuple-element.40), channel_id=1, source_target_pairs={{7,0},{8,1},{9,2},{10,3},{11,4},{12,5},{13,6},{14,7},{15,8},{16,9}... | collective-permute-start | bytes 3151880 | tf_op jit(solution)/shard_map/ppermute | solution.py:20
  479.2 32.1 %collective-permute-start.27 = (f32[114,2304]{1,0:T(8,128)S(1)}, f32[114,2304]{1,0:T(8,128)S(1)}, u32[]{:S(2)}, u32[]{:S(2)}) collective-permute-start(f32[114,2304]{1,0:T(8,128)S(1)} %get-tuple-element.41), channel_id=1, source_target_pairs={{0,7},{1,8},{2,9},{3,10},{4,11},{5,12},{6,13},{7,14},{8,15},{9,16}... | collective-permute-start | bytes 3151880 | tf_op jit(solution)/shard_map/ppermute | solution.py:20
  484.9 50.1 %collective-permute-start.26 = (f32[114,2304]{1,0:T(8,128)S(1)}, f32[114,2304]{1,0:T(8,128)S(1)}, u32[]{:S(2)}, u32[]{:S(2)}) collective-permute-start(f32[114,2304]{1,0:T(8,128)S(1)} %get-tuple-element.42), channel_id=1, source_target_pairs={{0,6},{1,7},{2,8},{3,9},{4,10},{5,11},{6,12},{7,13},{8,14},{9,15},... | collective-permute-start | bytes 3151880 | tf_op jit(solution)/shard_map/ppermute | solution.py:20
  486.2 66.8 %collective-permute-start.25 = (f32[114,2304]{1,0:T(8,128)S(1)}, f32[114,2304]{1,0:T(8,128)S(1)}, u32[]{:S(2)}, u32[]{:S(2)}) collective-permute-start(f32[114,2304]{1,0:T(8,128)S(1)} %get-tuple-element.43), channel_id=1, source_target_pairs={{0,5},{1,6},{2,7},{3,8},{4,9},{5,10},{6,11},{7,12},{8,13},{9,14},{... | collective-permute-start | bytes 3151880 | tf_op jit(solution)/shard_map/ppermute | solution.py:20
  487.6 89.3 %collective-permute-start.24 = (f32[114,2304]{1,0:T(8,128)}, f32[114,2304]{1,0:T(8,128)}, u32[]{:S(2)}, u32[]{:S(2)}) collective-permute-start(f32[114,2304]{1,0:T(8,128)} %get-tuple-element.44), channel_id=1, source_target_pairs={{0,4},{1,5},{2,6},{3,7},{4,8},{5,9},{6,10},{7,11},{8,12},{9,13},{1... | collective-permute-start | bytes 3151880 | tf_op jit(solution)/shard_map/ppermute | solution.py:20
  495.9 57.1 %copy-start.24 = (f32[114,2304]{1,0:T(8,128)}, f32[114,2304]{1,0:T(8,128)S(1)}, u32[]{:S(2)}) copy-start(f32[114,2304]{1,0:T(8,128)S(1)} %collective-permute-done.14) | copy-start | bytes 3151876
  496.0 82.2 %collective-permute-start.23 = (f32[114,2304]{1,0:T(8,128)}, f32[114,2304]{1,0:T(8,128)}, u32[]{:S(2)}, u32[]{:S(2)}) collective-permute-start(f32[114,2304]{1,0:T(8,128)} %get-tuple-element.45), channel_id=1, source_target_pairs={{0,3},{1,4},{2,5},{3,6},{4,7},{5,8},{6,9},{7,10},{8,11},{9,12},{10... | collective-permute-start | bytes 3151880 | tf_op jit(solution)/shard_map/ppermute | solution.py:20
  511.3 41.8 %copy-start.25 = (f32[114,2304]{1,0:T(8,128)}, f32[114,2304]{1,0:T(8,128)S(1)}, u32[]{:S(2)}) copy-start(f32[114,2304]{1,0:T(8,128)S(1)} %collective-permute-done.27) | copy-start | bytes 3151876
  511.3 100.8 %collective-permute-start.22 = (f32[114,2304]{1,0:T(8,128)}, f32[114,2304]{1,0:T(8,128)}, u32[]{:S(2)}, u32[]{:S(2)}) collective-permute-start(f32[114,2304]{1,0:T(8,128)} %get-tuple-element.46), channel_id=1, source_target_pairs={{0,2},{1,3},{2,4},{3,5},{4,6},{5,7},{6,8},{7,9},{8,10},{9,11},{10,... | collective-permute-start | bytes 3151880 | tf_op jit(solution)/shard_map/ppermute | solution.py:20
  535.0 19.4 %copy-start.26 = (f32[114,2304]{1,0:T(8,128)}, f32[114,2304]{1,0:T(8,128)S(1)}, u32[]{:S(2)}) copy-start(f32[114,2304]{1,0:T(8,128)S(1)} %collective-permute-done.26) | copy-start | bytes 3151876
  535.0 78.4 %collective-permute-start.21 = (f32[114,2304]{1,0:T(8,128)}, f32[114,2304]{1,0:T(8,128)}, u32[]{:S(2)}, u32[]{:S(2)}) collective-permute-start(f32[114,2304]{1,0:T(8,128)} %get-tuple-element.47), channel_id=1, source_target_pairs={{0,1},{1,2},{2,3},{3,4},{4,5},{5,6},{6,7},{7,8},{8,9},{9,10},{10,1... | collective-permute-start | bytes 3151880 | tf_op jit(solution)/shard_map/ppermute | solution.py:20
  553.1 61.6 %collective-permute-start.20 = (f32[114,2304]{1,0:T(8,128)}, f32[114,2304]{1,0:T(8,128)}, u32[]{:S(2)}, u32[]{:S(2)}) collective-permute-start(f32[114,2304]{1,0:T(8,128)} %get-tuple-element.48), channel_id=1, source_target_pairs={{1,0},{2,1},{3,2},{4,3},{5,4},{6,5},{7,6},{8,7},{9,8},{10,9},{11,1... | collective-permute-start | bytes 3151880 | tf_op jit(solution)/shard_map/ppermute | solution.py:20
  556.3 164.0 %all-gather.37.cloned.1.call-start = ((), (), s32[]{:S(2)}) async-start(), calls=%async_computation.15 | async-start | bytes 1382400 | tf_op jit(solution)/shard_map/all_gather | solution.py:54
  576.9 57.4 %collective-permute-start.19 = (f32[114,2304]{1,0:T(8,128)}, f32[114,2304]{1,0:T(8,128)}, u32[]{:S(2)}, u32[]{:S(2)}) collective-permute-start(f32[114,2304]{1,0:T(8,128)} %get-tuple-element.49), channel_id=1, source_target_pairs={{2,0},{3,1},{4,2},{5,3},{6,4},{7,5},{8,6},{9,7},{10,8},{11,9},{12,... | collective-permute-start | bytes 3151880 | tf_op jit(solution)/shard_map/ppermute | solution.py:20
  578.2 56.5 %collective-permute-start.18 = (f32[114,2304]{1,0:T(8,128)}, f32[114,2304]{1,0:T(8,128)}, u32[]{:S(2)}, u32[]{:S(2)}) collective-permute-start(f32[114,2304]{1,0:T(8,128)} %get-tuple-element.50), channel_id=1, source_target_pairs={{3,0},{4,1},{5,2},{6,3},{7,4},{8,5},{9,6},{10,7},{11,8},{12,9},{13... | collective-permute-start | bytes 3151880 | tf_op jit(solution)/shard_map/ppermute | solution.py:20
  612.1 83.9 %collective-permute-start.17 = (f32[114,2304]{1,0:T(8,128)}, f32[114,2304]{1,0:T(8,128)}, u32[]{:S(2)}, u32[]{:S(2)}) collective-permute-start(f32[114,2304]{1,0:T(8,128)} %get-tuple-element.51), channel_id=1, source_target_pairs={{4,0},{5,1},{6,2},{7,3},{8,4},{9,5},{10,6},{11,7},{12,8},{13,9},{1... | collective-permute-start | bytes 3151880 | tf_op jit(solution)/shard_map/ppermute | solution.py:20
  613.4 84.0 %collective-permute-start.16 = (f32[114,2304]{1,0:T(8,128)}, f32[114,2304]{1,0:T(8,128)}, u32[]{:S(2)}, u32[]{:S(2)}) collective-permute-start(f32[114,2304]{1,0:T(8,128)} %get-tuple-element.52), channel_id=1, source_target_pairs={{5,0},{6,1},{7,2},{8,3},{9,4},{10,5},{11,6},{12,7},{13,8},{14,9},{... | collective-permute-start | bytes 3151880 | tf_op jit(solution)/shard_map/ppermute | solution.py:20
  614.7 82.6 %collective-permute-start.15 = (f32[114,2304]{1,0:T(8,128)}, f32[114,2304]{1,0:T(8,128)}, u32[]{:S(2)}, u32[]{:S(2)}) collective-permute-start(f32[114,2304]{1,0:T(8,128)} %get-tuple-element.53), channel_id=1, source_target_pairs={{6,0},{7,1},{8,2},{9,3},{10,4},{11,5},{12,6},{13,7},{14,8},{15,9},... | collective-permute-start | bytes 3151880 | tf_op jit(solution)/shard_map/ppermute | solution.py:20
  623.8 81.3 %copy-start.12 = (bf16[114,1152]{1,0:T(8,128)(2,1)S(1)}, bf16[114,1152]{1,0:T(8,128)(2,1)}, u32[]{:S(2)}) copy-start(bf16[114,1152]{1,0:T(8,128)(2,1)} %param.15) | copy-start | bytes 787972
  623.8 81.3 %copy-start.40 = (f32[1152]{0:T(1024)S(1)}, f32[1152]{0:T(1024)}, u32[]{:S(2)}) copy-start(f32[1152]{0:T(1024)} %param.18) | copy-start | bytes 13828
  623.8 81.3 %copy-start.49 = (f32[114]{0:T(128)S(1)}, f32[114]{0:T(128)}, u32[]{:S(2)}) copy-start(f32[114]{0:T(128)} %copy-done.48) | copy-start | bytes 1372
  623.8 81.3 %copy-start.51 = (f32[114]{0:T(128)S(1)}, f32[114]{0:T(128)}, u32[]{:S(2)}) copy-start(f32[114]{0:T(128)} %copy-done.50) | copy-start | bytes 1372
  623.8 173.0 %all-gather.33.cloned.1.call-start = ((), (), s32[]{:S(2)}) async-start(), calls=%async_computation.13 | async-start | bytes 1382400 | tf_op jit(solution)/shard_map/all_gather | solution.py:52
  711.2 116.7 %all-gather.31.cloned.1.call-start = ((), (), s32[]{:S(2)}) async-start(), calls=%async_computation.12 | async-start | bytes 4147200 | tf_op jit(solution)/shard_map/all_gather | solution.py:51
  712.4 134.7 %all-gather.45.cloned.1.call-start = ((), (), s32[]{:S(2)}) async-start(), calls=%async_computation.19 | async-start | bytes 1382400 | tf_op jit(solution)/shard_map/all_gather | solution.py:54
  713.2 169.7 %all-gather.43.cloned.1.call-start = ((), (), s32[]{:S(2)}) async-start(), calls=%async_computation.18 | async-start | bytes 5222400 | tf_op jit(solution)/shard_map/all_gather | solution.py:53
  716.7 185.4 %all-gather.41.cloned.1.call-start = ((), (), s32[]{:S(2)}) async-start(), calls=%async_computation.17 | async-start | bytes 1382400 | tf_op jit(solution)/shard_map/all_gather | solution.py:52
  717.4 220.5 %all-gather.39.cloned.1.call-start = ((), (), s32[]{:S(2)}) async-start(), calls=%async_computation.16 | async-start | bytes 5222400 | tf_op jit(solution)/shard_map/all_gather | solution.py:51
  718.6 290.1 %reduce-scatter.7.cloned.1.call-start = ((), (), s32[]{:S(2)}) async-start(), calls=%async_computation.7 | async-start | bytes 1990656 | tf_op jit(solution)/shard_map/reduce_scatter | solution.py:70
  724.0 375.5 %reduce-scatter.5.cloned.1.call-start = ((), (), s32[]{:S(2)}) async-start(), calls=%async_computation.6 | async-start | bytes 4644864 | tf_op jit(solution)/shard_map/reduce_scatter | solution.py:69
  835.5 372.2 %reduce-scatter.11.cloned.1.call-start = ((), (), s32[]{:S(2)}) async-start(), calls=%async_computation.9 | async-start | bytes 5971968 | tf_op jit(solution)/shard_map/reduce_scatter | solution.py:70
  894.3 421.5 %reduce-scatter.9.cloned.1.call-start = ((), (), s32[]{:S(2)}) async-start(), calls=%async_computation.8 | async-start | bytes 5971968 | tf_op jit(solution)/shard_map/reduce_scatter | solution.py:69
  (37 other events, 235.3 us)
Sparse Core Ops, SparseCore 0:
  9.5 58.5 all-gather.22
  69.7 59.2 all-gather.24
  130.6 116.8 all-gather.26
  248.8 68.6 all-gather.28
  556.4 44.5 all-gather.34
  623.9 48.2 all-gather.36
  711.4 85.4 all-gather.32
  798.4 29.4 all-gather.30
  830.0 17.0 all-gather.44
  848.5 34.3 all-gather.42
  885.0 17.0 all-gather.40
  903.5 34.3 all-gather.38
  942.0 66.7 reduce-scatter.6
  1012.7 86.7 reduce-scatter.4
  1103.5 104.1 reduce-scatter.10
  1211.7 104.1 reduce-scatter.8
where the time goes:
time: 1330 us; the launch traced here: 1320 us
  waiting for transfers between devices  806 us (61%)
  local copies, waits for them, and re-layouts  178 us (13%)
  starting transfers between devices  123 us (9%)
  matrix products  99.8 us (8%)
  other arithmetic  55.2 us (4%)
  blocking collectives  42.1 us (3%)
  between operations  18.5 us (1%)
    ppermute x28, waiting for transfers between devices, passed_along(): return lax.ppermute(block, axis, route)  245 us
    reduce_scatter x2, waiting for transfers between devices, replica_sums(): lax.psum_scatter(first_rows, 'rep', scatter_dimension=1, tiled=True)  199 us
    ppermute x28, starting transfers between devices, passed_along(): return lax.ppermute(block, axis, route)  122 us
    reduce_scatter x2, waiting for transfers between devices, replica_sums(): lax.psum_scatter(second_rows, 'rep', scatter_dimension=1, tiled=True)  117 us
    all_gather x2, waiting for transfers between devices, owned_grads(): lax.all_gather(right_one, 'grp', axis=0, tiled=True)  80.5 us
    all_gather x2, waiting for transfers between devices, owned_grads(): lax.all_gather(left_one, 'grp', axis=0, tiled=True)  62.8 us
    concatenate x1, local copies, waits for them, and re-layouts, per_device(): neighbours = jnp.concatenate(pieces, axis=0)  57.9 us
    unnamed x125, local copies, waits for them, and re-layouts  53.1 us
  transfers between devices with their start and end apart: 44, of which 26 were waited for; matrix products, arithmetic and copies ran while one was open for 16% of the time, Pallas kernels for 0%

commit v1 on v0

v1 whole, which is shorter than its diff:
```python
import functools

import jax
import jax.numpy as jnp
from jax import lax
from jax.experimental import pallas as pl
from jax.sharding import PartitionSpec as P

H = 16
HD = 72
IMG = 729


EPSILON = 1e-06
SQRT_TWO_PI = 0.7978845608028654
CUBIC = 0.044715
NEGATIVE = -1e30


def norm_forward(rows, gain_row, shift_row):
    centered = rows - jnp.mean(rows, axis=-1, keepdims=True)
    inverse = lax.rsqrt(jnp.mean(centered * centered, axis=-1, keepdims=True) + EPSILON)
    normed = centered * inverse
    return (normed, inverse, normed * gain_row + shift_row)


def norm_backward(dscaled, normed, inverse, gain_row):
    dnormed = dscaled * gain_row
    return inverse * (
        dnormed
        - jnp.mean(dnormed, axis=-1, keepdims=True)
        - normed * jnp.mean(dnormed * normed, axis=-1, keepdims=True)
    )


def gelu_parts(before):
    inside = SQRT_TWO_PI * (before + CUBIC * before * before * before)
    tangent = jnp.tanh(inside)
    activated = 0.5 * before * (1.0 + tangent)
    derivative = 0.5 * (1.0 + tangent) + 0.5 * before * (1.0 - tangent * tangent) * SQRT_TWO_PI * (
        1.0 + 3.0 * CUBIC * before * before
    )
    return (activated, derivative)


def dot_over(left, right, left_axis, right_axis):
    return lax.dot_general(
        left, right, (((left_axis,), (right_axis,)), ((), ())), preferred_element_type=jnp.float32
    )


def forward_kernel(q_ref, k_ref, v_ref, qi_ref, ki_ref, mixed_ref, lse_ref):
    allowed = qi_ref[0] == ki_ref[0]
    raw = dot_over(q_ref[0], k_ref[0], 1, 1) * (HD ** (-0.5))
    scores = jnp.where(allowed, raw, NEGATIVE)
    highest = jnp.max(scores, axis=-1, keepdims=True)
    powers = jnp.where(allowed, jnp.exp(scores - highest), 0.0)
    total = jnp.sum(powers, axis=-1, keepdims=True)
    total = jnp.where(total > 0.0, total, 1.0)
    weights = (powers * (1.0 / total)).astype(jnp.bfloat16)
    mixed_ref[0] = dot_over(weights, v_ref[0], 1, 0).astype(jnp.bfloat16)
    lse_ref[0] = highest + jnp.log(total)


def backward_kernel(
    q_ref, k_ref, v_ref, qi_ref, ki_ref, mixed_ref, lse_ref, dmixed_ref, dq_ref, dk_ref, dv_ref
):
    allowed = qi_ref[0] == ki_ref[0]
    raw = dot_over(q_ref[0], k_ref[0], 1, 1) * (HD ** (-0.5))
    probs = jnp.where(allowed, jnp.exp(jnp.where(allowed, raw - lse_ref[0], 0.0)), 0.0)
    dmixed = dmixed_ref[0]
    delta = jnp.sum(
        dmixed.astype(jnp.float32) * mixed_ref[0].astype(jnp.float32), axis=-1, keepdims=True
    )
    dprob = dot_over(dmixed, v_ref[0], 1, 1)
    dscore = (probs * (dprob - delta) * (HD ** (-0.5))).astype(jnp.bfloat16)
    dq_ref[0] = dot_over(dscore, k_ref[0], 1, 0)
    dk_ref[0] = dot_over(dscore, q_ref[0], 0, 0)
    dv_ref[0] = dot_over(probs.astype(jnp.bfloat16), dmixed, 0, 0)


def blocked(shape):
    return pl.BlockSpec((1,) + shape[1:], lambda b: (b, 0, 0))


def block_call(kernel, args, outs):
    return pl.pallas_call(
        kernel,
        grid=(args[0].shape[0],),
        in_specs=[blocked(a.shape) for a in args],
        out_specs=[blocked(o.shape) for o in outs],
        out_shape=outs,
    )(*args)


def per_device(
    tokens,
    cotangent,
    slice_sizes,
    gain_one,
    shift_one,
    attn_in,
    attn_bias,
    attn_out,
    out_bias,
    gain_two,
    shift_two,
    mlp_up,
    up_bias,
    mlp_down,
    down_bias,
):
    capacity, width = tokens.shape
    reps, groups = lax.axis_size("rep"), lax.axis_size("grp")
    devices = reps * groups
    turns = H // groups
    segments = reps // turns
    reach = (IMG - 2 + capacity - 1) // (capacity - 1)
    rows = groups * capacity
    halo = reach * capacity
    segment_rows = H * capacity
    window = rows + 2 * halo
    rep, member = lax.axis_index("rep"), lax.axis_index("grp")
    device = rep * groups + member
    segment, turn = rep // turns, rep % turns
    head = member * turns + turn
    kinds = attn_in.shape[0] // HD
    rep_sets = [[s * turns + i for i in range(turns)] for s in range(segments)]
    all_sets = [[s * H + i for i in range(H)] for s in range(segments)]
    spread = functools.partial(
        lax.all_to_all, split_axis=0, concat_axis=0, tiled=True
    )

    def gathered(block):
        return lax.all_gather(block, "grp", axis=0, tiled=True)

    def scattered(partial_rows):
        blocks = partial_rows.astype(jnp.bfloat16).reshape(groups, capacity, width)
        return jnp.sum(spread(blocks, "grp").astype(jnp.float32), axis=0)

    def rep_summed(grad_rows):
        return lax.psum_scatter(
            grad_rows.astype(jnp.bfloat16), "rep", scatter_dimension=1, tiled=True
        ).astype(jnp.float32)

    starts = jnp.cumsum(slice_sizes) - slice_sizes
    own_count = slice_sizes[device]
    row_index = jnp.arange(capacity, dtype=jnp.int32)
    live_col = (row_index < own_count)[:, None]

    images = jnp.where(
        row_index[None, :] < slice_sizes[:, None],
        (starts[:, None] + row_index[None, :]) // IMG,
        -2,
    )
    padding = jnp.full((reach, capacity), -2, jnp.int32)
    images = jnp.concatenate([padding, images, padding], axis=0)
    images = lax.dynamic_slice_in_dim(images, segment * H, H + 2 * reach, 0).reshape(-1)
    query_image = images[halo : halo + segment_rows]
    query_image = jnp.where(query_image < 0, -1, query_image).reshape(turns, rows, 1)

    def windows(whole):
        return jnp.stack([whole[b * rows : b * rows + window] for b in range(turns)])

    key_image = windows(images).reshape(turns, 1, window)

    dfinal_b = jnp.where(live_col, cotangent, jnp.zeros_like(cotangent))
    dfinal = dfinal_b.astype(jnp.float32)
    tokens_f = tokens.astype(jnp.float32)
    group_normed, _, group_scaled = norm_forward(
        gathered(tokens).astype(jnp.float32), gain_one, shift_one
    )
    first = group_scaled.astype(jnp.bfloat16)
    normed_one, inverse_one, _ = norm_forward(tokens_f, gain_one, shift_one)
    dfinal_all = gathered(dfinal_b)
    bias_full = jnp.concatenate([attn_bias[0], jnp.zeros((width,), jnp.float32), attn_bias[1]])
    own_bias = lax.dynamic_slice_in_dim(bias_full, member * kinds * HD, kinds * HD, 0)
    projected = (dot_over(first, attn_in, 1, 1) + own_bias).astype(jnp.bfloat16)
    padded = jnp.pad(projected, ((0, 0), (0, (H - kinds) * HD)))
    shift = (member * kinds) % H
    rolled = lax.dynamic_slice_in_dim(
        jnp.concatenate([padded, padded], axis=1), ((H - shift) % H) * HD, H * HD, 1
    )
    outgoing = rolled.reshape(rows, groups, turns, HD).transpose(2, 1, 0, 3)
    incoming = spread(
        outgoing.reshape(H, rows, HD), ("rep", "grp"), axis_index_groups=all_sets
    ).reshape(turns, groups, rows, HD)

    def kind_of(kind):
        return lax.dynamic_index_in_dim(incoming, (kind * H + head) // kinds, 1, keepdims=False)

    queries = kind_of(0)
    keyvalue = jnp.concatenate([kind_of(1), kind_of(2)], axis=-1).reshape(segment_rows, 2 * HD)
    onward = [(r, r + turns) for r in range(reps - turns)]
    backward = [(r + turns, r) for r in range(reps - turns)]
    before_rows = lax.ppermute(keyvalue[segment_rows - halo :], "rep", onward)
    after_rows = lax.ppermute(keyvalue[:halo], "rep", backward)
    neighbours = jnp.concatenate([before_rows, keyvalue, after_rows], axis=0)
    keys = windows(neighbours[:, :HD])
    values = windows(neighbours[:, HD:])
    shared = (queries, keys, values, query_image, key_image)
    mixed, lse = block_call(
        forward_kernel,
        shared,
        [
            jax.ShapeDtypeStruct((turns, rows, HD), jnp.bfloat16),
            jax.ShapeDtypeStruct((turns, rows, 1), jnp.float32),
        ],
    )
    mixed_own = (
        spread(mixed, "rep", axis_index_groups=rep_sets)
        .transpose(1, 0, 2)
        .reshape(rows, turns * HD)
    )
    resid = tokens_f + scattered(dot_over(mixed_own, attn_out, 1, 0)) + out_bias
    normed_two, inverse_two, scaled_two = norm_forward(resid, gain_two, shift_two)
    second = gathered(scaled_two.astype(jnp.bfloat16))
    hidden_rows = mlp_up.shape[0]
    own_up_bias = lax.dynamic_slice_in_dim(up_bias, member * hidden_rows, hidden_rows, 0)
    before = dot_over(second, mlp_up, 1, 1) + own_up_bias
    activated, derivative = gelu_parts(before)
    hidden = activated.astype(jnp.bfloat16)
    dbefore = dot_over(dfinal_all, mlp_down, 1, 1) * derivative
    dbefore_b = dbefore.astype(jnp.bfloat16)
    dsecond = scattered(dot_over(dbefore_b, mlp_up, 1, 0))
    dresid = dfinal + norm_backward(dsecond, normed_two, inverse_two, gain_two)
    dresid_all = gathered(dresid.astype(jnp.bfloat16))
    dmixed_own = dot_over(dresid_all, attn_out, 1, 1).astype(jnp.bfloat16)
    dmixed = spread(
        dmixed_own.reshape(rows, turns, HD).transpose(1, 0, 2), "rep", axis_index_groups=rep_sets
    )
    final = resid + scattered(dot_over(hidden, mlp_down, 1, 0)) + down_bias
    block_output = jnp.where(live_col, final, 0.0).astype(jnp.bfloat16)
    summed = rep_summed(
        jnp.concatenate(
            [
                dot_over(dbefore_b, second, 0, 0).astype(jnp.bfloat16),
                dot_over(hidden, dfinal_all, 0, 0).astype(jnp.bfloat16),
                dot_over(mixed_own, dresid_all, 0, 0).astype(jnp.bfloat16),
            ],
            axis=0,
        )
    )
    dmlp_up = summed[:hidden_rows]
    dmlp_down = summed[hidden_rows : 2 * hidden_rows]
    dattn_out = summed[2 * hidden_rows :]

    dq, dk, dv = block_call(
        backward_kernel,
        shared + (mixed, lse, dmixed),
        [
            jax.ShapeDtypeStruct((turns, rows, HD), jnp.float32),
            jax.ShapeDtypeStruct((turns, window, HD), jnp.float32),
            jax.ShapeDtypeStruct((turns, window, HD), jnp.float32),
        ],
    )
    dkv = jnp.concatenate([dk, dv], axis=-1)
    span = segment_rows + 2 * halo
    dneighbours = sum(
        jnp.pad(dkv[b], ((b * rows, span - window - b * rows), (0, 0))) for b in range(turns)
    )
    to_before = lax.ppermute(dneighbours[:halo].astype(jnp.bfloat16), "rep", backward)
    to_after = lax.ppermute(dneighbours[halo + segment_rows :].astype(jnp.bfloat16), "rep", onward)
    dkeyvalue = (
        dneighbours[halo : halo + segment_rows]
        + jnp.pad(to_before.astype(jnp.float32), ((segment_rows - halo, 0), (0, 0)))
        + jnp.pad(to_after.astype(jnp.float32), ((0, segment_rows - halo), (0, 0)))
    ).astype(jnp.bfloat16)
    dqkv = jnp.stack(
        [
            dq.astype(jnp.bfloat16),
            dkeyvalue[:, :HD].reshape(turns, rows, HD),
            dkeyvalue[:, HD:].reshape(turns, rows, HD),
            jnp.zeros((turns, rows, HD), jnp.bfloat16),
        ]
    )
    pieces = []
    for g in range(groups):
        kind = (g * kinds - head + H - 1) // H
        fits = (kind * H + head < (g + 1) * kinds) & (kind < 3)
        pieces.append(
            lax.dynamic_index_in_dim(dqkv, jnp.where(fits, kind, 3), 0, keepdims=False)
        )
    outgoing = jnp.stack(pieces, axis=1).reshape(H, rows, HD)
    incoming = spread(outgoing, ("rep", "grp"), axis_index_groups=all_sets)
    by_head = (
        incoming.reshape(turns, groups, rows, HD).transpose(2, 1, 0, 3).reshape(rows, H * HD)
    )
    dprojected = lax.dynamic_slice_in_dim(
        jnp.concatenate([by_head, by_head], axis=1), shift * HD, kinds * HD, 1
    )
    dattn_in = rep_summed(dot_over(dprojected, first, 0, 0))
    dfirst_partial = dot_over(dprojected, attn_in, 1, 0)
    dfirst = scattered(dfirst_partial)
    input_grad = jnp.where(
        live_col, dresid + norm_backward(dfirst, normed_one, inverse_one, gain_one), 0.0
    )
    dbias = jnp.stack([jnp.sum(dq, axis=(0, 1)), jnp.sum(dv, axis=(0, 1))])
    dattn_bias = lax.dynamic_update_slice_in_dim(
        jnp.zeros((2, width), jnp.float32), dbias, head * HD, 1
    )
    dup_bias = lax.dynamic_update_slice_in_dim(
        jnp.zeros(up_bias.shape, jnp.float32), jnp.sum(dbefore, axis=0), member * hidden_rows, 0
    )
    dgain_one, dshift_one, dattn_bias, dout_bias, dgain_two, dshift_two, dup_bias, ddown_bias = (
        lax.psum(
            (
                jnp.sum(dfirst_partial * group_normed, axis=0),
                jnp.sum(dfirst_partial, axis=0),
                dattn_bias,
                jnp.sum(dresid, axis=0),
                jnp.sum(dsecond * normed_two, axis=0),
                jnp.sum(dsecond, axis=0),
                dup_bias,
                jnp.sum(dfinal, axis=0),
            ),
            ("rep", "grp"),
        )
    )
    return (
        block_output,
        input_grad,
        dgain_one,
        dshift_one,
        dattn_in,
        dattn_bias,
        dattn_out,
        dout_bias,
        dgain_two,
        dshift_two,
        dmlp_up,
        dup_bias,
        dmlp_down,
        ddown_bias,
    )


def solution(mesh):
    in_specs = (
        P(("rep", "grp"), None),
        P(("rep", "grp"), None),
        P(),
        P(),
        P(),
        P("grp", None),
        P(),
        P("grp", None),
        P(),
        P(),
        P(),
        P("grp", None),
        P(),
        P("grp", None),
        P(),
    )
    out_specs = (
        P(("rep", "grp"), None),
        P(("rep", "grp"), None),
        P(),
        P(),
        P("grp", "rep"),
        P(),
        P("grp", "rep"),
        P(),
        P(),
        P(),
        P("grp", "rep"),
        P(),
        P("grp", "rep"),
        P(),
    )
    return jax.shard_map(
        per_device, mesh=mesh, in_specs=in_specs, out_specs=out_specs, check_vma=False
    )
```

time: 1330 us -> 561 us (0.42)
  waiting for transfers between devices: 806 us -> 230 us
  local copies, waits for them, and re-layouts: 178 us -> 94.9 us
  starting transfers between devices: 123 us -> 42.5 us
  matrix products: 99.8 us -> 37.8 us
  Pallas kernels: 0 us -> 33.6 us
  blocking collectives: 42.1 us -> 59 us
  other arithmetic: 55.2 us -> 40.3 us
    reduce_scatter x4 -> x1, waiting for transfers between devices: 316 us -> 0.01 us  [rep_summed(): lax.psum_scatter(grad_rows.astype(jnp.bfloat16), 'rep', scatter_dimension...]
    ppermute x28 -> x4, waiting for transfers between devices: 245 us -> 32.2 us  [the longest x1 14.5 us: per_device(): lax.ppermute(dneighbours[:halo].astype(jnp.bfloat16), 'rep', backward)]
    all_gather x12 -> x4, waiting for transfers between devices: 242 us -> 50.7 us  [gathered(): return lax.all_gather(block, 'grp', axis=0, tiled=True)]
    ppermute x28 -> x4, starting transfers between devices: 122 us -> 13.7 us  [the longest x1 5.49 us: per_device(): lax.ppermute(dneighbours[halo + segment_rows:].astype(jnp.bfloat16), 'rep...]
    all_to_all x0 -> x7, waiting for transfers between devices: none -> 75.4 us  [the longest x4 38.3 us: scattered(): return jnp.sum(spread(blocks, 'grp').astype(jnp.float32), axis=0)]
    unnamed x16 -> x7, waiting for transfers between devices: 3.41 us -> 71.8 us
    dot_general x18 -> x12, matrix products: 99.8 us -> 37.8 us  [dot_over(): lax.dot_general(left, right, (((left_axis,), (right_axis,)), ((), ())), p...]
    pallas_call x0 -> x2, Pallas kernels: none -> 33.6 us  [block_call(): pl.pallas_call(kernel, grid=(args[0].shape[0],), in_specs=[blocked(a.shap...]
  transfers between devices with their start and end apart: 44 -> 17, of which waited for: 26 -> 13; matrix products, arithmetic and copies ran while one was open for 16% -> 15% of each run, Pallas kernels for 0% -> 0%
where the time goes in v1:
time: 561 us; the launch traced here: 554 us
  waiting for transfers between devices  230 us (41%)
  local copies, waits for them, and re-layouts  94.9 us (17%)
  blocking collectives  59 us (11%)
  starting transfers between devices  42.5 us (8%)
  other arithmetic  40.3 us (7%)
  matrix products  37.8 us (7%)
  Pallas kernels  33.6 us (6%)
  between operations  15.5 us (3%)
    unnamed x7, waiting for transfers between devices  71.8 us
    all_gather x4, waiting for transfers between devices, gathered(): return lax.all_gather(block, 'grp', axis=0, tiled=True)  50.7 us
    psum x1, blocking collectives, per_device(): lax.psum((jnp.sum(dfirst_partial * group_normed, axis=0), jnp.sum(dfirst_...  48.6 us
    all_to_all x4, waiting for transfers between devices, scattered(): return jnp.sum(spread(blocks, 'grp').astype(jnp.float32), axis=0)  38.3 us
    dot_general x12, matrix products, dot_over(): lax.dot_general(left, right, (((left_axis,), (right_axis,)), ((), ())), p...  37.8 us
    pallas_call x2, Pallas kernels, block_call(): pl.pallas_call(kernel, grid=(args[0].shape[0],), in_specs=[blocked(a.shap...  33.6 us
    concatenate x1, local copies, waits for them, and re-layouts, per_device(): jnp.concatenate([dot_over(dbefore_b, second, 0, 0).astype(jnp.bfloat16),...  28 us
    unnamed x74, local copies, waits for them, and re-layouts  26.3 us
  transfers between devices with their start and end apart: 17, of which 13 were waited for; matrix products, arithmetic and copies ran while one was open for 15% of the time, Pallas kernels for 0%

profile of v1, /device:TPU:0, one launch (start us, length us, event | category | flops | bytes accessed | tf_op | source)
XLA Modules:
  0.0 553.6 jit_solution(14904815456541559069)
XLA Ops:
  8.9 20.5 %all-gather.9.cloned.1.call-done = bf16[4,114,1152]{2,1,0:T(8,128)(2,1)} async-done(((bf16[1,114,1152]{2,1,0:T(8,128)(2,1)}), bf16[4,114,1152]{2,1,0:T(8,128)(2,1)}) %all-gather.9.cloned.1.call-update) | async-done | bytes 1050640 | tf_op jit(solution)/shard_map/all_gather | solution.py:135
  30.9 2.9 reshape.221
  33.8 2.1 multiply_reduce_fusion.1
  36.0 3.2 add_convert_fusion.1
  41.9 2.4 copy.66
  44.3 4.4 all-to-all-start
  51.5 14.8 %all-to-all-done = bf16[16,456,72]{1,2,0:T(8,128)(2,1)} async-done(((bf16[16,456,72]{1,2,0:T(8,128)(2,1)}), bf16[16,456,72]{1,2,0:T(8,128)(2,1)}, u32[]{:S(2)}, u32[]{:S(2)}) %all-to-all-start) | async-done | bytes 1050656 | tf_op jit(solution)/shard_map/all_to_all | solution.py:185
  66.3 2.0 constant_dynamic-slice_fusion.5
  71.1 5.1 collective-permute-start
  79.0 1.9 copy.67
  80.9 3.3 collective-permute-done
  84.2 14.4 %collective-permute-done.1 = bf16[798,144]{1,0:T(8,128)(2,1)} collective-permute-done((bf16[798,144]{1,0:T(8,128)(2,1)}, bf16[798,144]{1,0:T(8,128)(2,1)}, u32[]{:S(2)}, u32[]{:S(2)}) %collective-permute-start.1) | collective-permute-done | bytes 229856 | tf_op jit(solution)/shard_map/ppermute | solution.py:197
  98.6 2.2 maximum_maximum_fusion.1
  102.2 1.9 pad_maximum_fusion.2.v_ref
  104.0 2.0 pad_maximum_fusion.1.k_ref
  106.1 16.3 %shard_map.254 = (bf16[4,456,72]{2,1,0:T(8,128)(2,1)}, f32[4,456,1]{2,1,0:T(8,128)}) custom-call(bf16[4,456,72]{2,1,0:T(8,128)(2,1)} %bitcast.88, bf16[4,2052,72]{2,1,0:T(8,128)(2,1)} %pad_maximum_fusion.1.k_ref, bf16[4,2052,72]{2,1,0:T(8,128)(2,1)} %pad_maximum_fusion.2.v_ref, s32[4,456,1]{2,1,0:T(8,128)} %compare_select_fusion.qi_ref, ...), custom_call_target="tpu_custom_call" | custom-call | tf_op jit(solution)/shard_map/pallas_call | solution.py:87
  122.4 1.9 copy.73
  124.3 3.5 all-to-all-start.1
  129.0 4.8 all-to-all-done.1
  133.8 1.8 convolution_convert_fusion.3
  135.6 2.6 reshape.205
  138.2 4.4 all-to-all-start.2
  142.6 1.8 fusion.36
  144.8 17.3 %all-to-all-done.2 = bf16[4,114,1152]{2,1,0:T(8,128)(2,1)} async-done(((bf16[4,114,1152]{2,1,0:T(8,128)(2,1)}), bf16[4,114,1152]{2,1,0:T(8,128)(2,1)}, u32[]{:S(2)}, u32[]{:S(2)}) %all-to-all-start.2) | async-done | bytes 1050656 | tf_op jit(solution)/shard_map/all_to_all | solution.py:139
  165.8 2.5 reshape.218
  168.3 13.0 %all-gather.11.cloned.1.call-done = bf16[4,114,1152]{2,1,0:T(8,128)(2,1)} async-done(((bf16[1,114,1152]{2,1,0:T(8,128)(2,1)}), bf16[4,114,1152]{2,1,0:T(8,128)(2,1)}) %all-gather.11.cloned.1.call-update) | async-done | bytes 1050640 | tf_op jit(solution)/shard_map/all_gather | solution.py:135
  181.3 2.5 reshape.216
  183.8 3.8 convolution_add_fusion
  187.7 2.4 fusion.50
  191.0 2.8 convolution_convert_fusion.4
  193.8 2.6 reshape.207
  196.4 4.3 all-to-all-start.4
  200.7 4.6 convolution_convert_fusion.5
  205.3 2.5 reshape.206
  207.9 7.9 %all-to-all-done.4 = bf16[4,114,1152]{2,1,0:T(8,128)(2,1)} async-done(((bf16[4,114,1152]{2,1,0:T(8,128)(2,1)}), bf16[4,114,1152]{2,1,0:T(8,128)(2,1)}, u32[]{:S(2)}, u32[]{:S(2)}) %all-to-all-start.4) | async-done | bytes 1050656 | tf_op jit(solution)/shard_map/all_to_all | solution.py:139
  215.8 3.5 all-to-all-start.3
  221.3 13.0 %all-to-all-done.3 = bf16[4,114,1152]{2,1,0:T(8,128)(2,1)S(1)} async-done(((bf16[4,114,1152]{2,1,0:T(8,128)(2,1)}), bf16[4,114,1152]{2,1,0:T(8,128)(2,1)S(1)}, u32[]{:S(2)}, u32[]{:S(2)}) %all-to-all-start.3) | async-done | bytes 1050656 | tf_op jit(solution)/shard_map/all_to_all | solution.py:139
  236.4 17.2 %all-gather.15.cloned.1.call-done = bf16[4,114,1152]{2,1,0:T(8,128)(2,1)} async-done(((bf16[1,114,1152]{2,1,0:T(8,128)(2,1)}), bf16[4,114,1152]{2,1,0:T(8,128)(2,1)}) %all-gather.15.cloned.1.call-update) | async-done | bytes 1050640 | tf_op jit(solution)/shard_map/all_gather | solution.py:135
  255.2 2.0 convolution_convert_fusion.7
  257.2 10.4 %all_to_all.40 = bf16[4,456,72]{1,2,0:T(8,128)(2,1)S(1)} all-to-all(bf16[4,456,72]{1,2,0:T(8,128)(2,1)S(1)} %bitcast.105), channel_id=1, replica_groups={{0,4,8,12},{16,20,24,28},{1,5,9,13},{17,21,25,29},{2,6,10,14},{18,22,26..., dimensions={0} | all-to-all | bytes 525312 | tf_op jit(solution)/shard_map/all_to_all | solution.py:229
  268.6 17.3 %shard_map.255 = (f32[4,456,72]{2,1,0:T(8,128)}, f32[4,2052,72]{2,1,0:T(8,128)}, f32[4,2052,72]{2,1,0:T(8,128)}) custom-call(bf16[4,456,72]{2,1,0:T(8,128)(2,1)} %bitcast.89, bf16[4,2052,72]{2,1,0:T(8,128)(2,1)} %pad_maximum_fusion.1.k_ref, bf16[4,2052,72]{2,1,0:T(8,128)(2,1)} %pad_maximum_fusion.2.v_ref, s32[4,456,1]{2,1,0:T(8,128)} %compare_select_fusion.qi_ref, ...), custom_call_target="tpu_custom_call" | custom-call | tf_op jit(solution)/shard_map/pallas_call | solution.py:87
  285.8 4.6 fusion.3
  290.5 2.7 fusion.42
  294.6 5.5 collective-permute-start.3
  300.6 14.5 %collective-permute-done.2 = bf16[798,144]{1,0:T(8,128)(2,1)S(1)} collective-permute-done((bf16[798,144]{1,0:T(8,128)(2,1)S(1)}, bf16[798,144]{1,0:T(8,128)(2,1)S(1)}, u32[]{:S(2)}, u32[]{:S(2)}) %collective-permute-start.2) | collective-permute-done | bytes 229856 | tf_op jit(solution)/shard_map/ppermute | solution.py:262
  315.1 1.9 fusion.13
  322.8 4.5 all-to-all-start.6
  327.4 17.6 %all-to-all-done.6 = bf16[16,456,72]{1,2,0:T(8,128)(2,1)} async-done(((bf16[16,456,72]{1,2,0:T(8,128)(2,1)}), bf16[16,456,72]{1,2,0:T(8,128)(2,1)}, u32[]{:S(2)}, u32[]{:S(2)}) %all-to-all-start.6) | async-done | bytes 1050656 | tf_op jit(solution)/shard_map/all_to_all | solution.py:285
  347.4 3.3 convolution_convert_fusion.2
  351.0 4.8 convolution_convert_fusion.1
  355.8 3.2 convolution_convert_fusion
  360.5 28.0 %concatenate.49 = bf16[2440,1152]{1,0:T(8,128)(2,1)} concatenate(bf16[1076,1152]{1,0:T(8,128)(2,1)} %convolution_convert_fusion.1, bf16[1076,1152]{1,0:T(8,128)(2,1)} %convolution_convert_fusion, bf16[288,1152]{1,0:T(8,128)(2,1)} %convolution_convert_fusion.6), dimensions={0} | concatenate | bytes 11243520 | tf_op jit(solution)/shard_map/concatenate | solution.py:235
  388.5 9.0 %copy.83 = bf16[2440,1152]{0,1:T(8,128)(2,1)} copy(bf16[2440,1152]{1,0:T(8,128)(2,1)} %concatenate.49) | data formatting | bytes 11243520
  397.5 4.5 fusion.40
  401.9 2.5 reshape.212
  404.5 3.5 all-to-all-start.7
  408.3 3.3 reduce_sum.224
  411.9 48.6 %all-reduce.7 = (f32[1152]{0:T(1024)}, f32[1152]{0:T(1024)}, f32[2,1152]{1,0:T(2,128)}, f32[1152]{0:T(1024)}, f32[1152]{0:T(1024)}, /*index=5*/f32[1152]{0:T(1024)}, f32[4304]{0:T(1024)}, f32[1152]{0:T(1024)}) all-reduce(f32[1152]{0:T(1024)S(1)} %get-tuple-element.81, ...), channel_id=1, replica_groups=mesh['rep'=8,'grp'=4] {'rep','grp'}, use_global_device_ids=true, to_apply=%region_16.17 | all-reduce | flops 13520 | bytes 108160 | tf_op jit(solution)/shard_map/psum | solution.py:306
  462.0 1.8 convert_element_type.121
  463.8 71.0 %reduce-scatter.7.cloned.1.call-done = bf16[144,2440]{1,0:T(8,128)(2,1)} async-done(((bf16[1152,2440]{1,0:T(8,128)(2,1)}), bf16[144,2440]{1,0:T(8,128)(2,1)}) %reduce-scatter.7.cloned.1.call-update) | async-done | bytes 702736
  534.8 1.8 copy.84
  537.7 3.0 fusion.46
  541.5 2.4 copy.82
  543.9 2.4 copy.81
  (161 shorter events, 44.1 us)
Async XLA Ops:
  7.2 180.5 %copy-start = (bf16[1076,1152]{1,0:T(8,128)(2,1)S(1)}, bf16[1076,1152]{1,0:T(8,128)(2,1)}, u32[]{:S(2)}) copy-start(bf16[1076,1152]{1,0:T(8,128)(2,1)} %param.28) | copy-start | bytes 7437316
  7.2 22.1 %all-gather.9.cloned.1.call-start = ((), (), s32[]{:S(2)}) async-start(), calls=%async_computation.11 | async-start | bytes 1382400 | tf_op jit(solution)/shard_map/all_gather | solution.py:135
  30.9 5.0 copy-start.20
  30.9 5.0 copy-start.28
  33.8 2.2 copy-start.3
  36.0 3.2 copy-start.25
  41.9 6.9 %copy-start.24 = (s32[32]{0:T(128)S(1)}, s32[32]{0:T(128)}, u32[]{:S(2)}) copy-start(s32[32]{0:T(128)} %param.17) | copy-start | bytes 388
  44.3 22.0 %all-to-all-start = ((bf16[16,456,72]{1,2,0:T(8,128)(2,1)}), bf16[16,456,72]{1,2,0:T(8,128)(2,1)}, u32[]{:S(2)}, u32[]{:S(2)}) async-start(bf16[16,456,72]{1,2,0:T(8,128)(2,1)} %bitcast.86), calls=%async_computation | async-start | bytes 2359296 | tf_op jit(solution)/shard_map/all_to_all | solution.py:185
  69.8 8.1 %copy-start.10 = (s32[4,456,1]{2,1,0:T(8,128)S(1)}, s32[4,456,1]{2,1,0:T(8,128)}, u32[]{:S(2)}) copy-start(s32[4,456,1]{2,1,0:T(8,128)} %slice.144) | copy-start | bytes 21892
  71.1 13.1 %collective-permute-start = (bf16[798,144]{1,0:T(8,128)(2,1)}, bf16[798,144]{1,0:T(8,128)(2,1)}, u32[]{:S(2)}, u32[]{:S(2)}) collective-permute-start(bf16[798,144]{1,0:T(8,128)(2,1)} %get-tuple-element.135), channel_id=1, source_target_pairs={{0,16},{4,20},{8,24},{12,28},{1,17},{5,21},{9,25},{13,29},{2,18},{... | collective-permute-start | bytes 689480 | tf_op jit(solution)/shard_map/ppermute | solution.py:196
  76.2 22.4 %collective-permute-start.1 = (bf16[798,144]{1,0:T(8,128)(2,1)}, bf16[798,144]{1,0:T(8,128)(2,1)}, u32[]{:S(2)}, u32[]{:S(2)}) collective-permute-start(bf16[798,144]{1,0:T(8,128)(2,1)} %get-tuple-element.136), channel_id=1, source_target_pairs={{16,0},{20,4},{24,8},{28,12},{17,1},{21,5},{25,9},{29,13},{18,2},{... | collective-permute-start | bytes 689480 | tf_op jit(solution)/shard_map/ppermute | solution.py:197
  106.1 27.8 %copy-start.18 = (bf16[288,1152]{1,0:T(8,128)(2,1)S(1)}, bf16[288,1152]{1,0:T(8,128)(2,1)}, u32[]{:S(2)}) copy-start(bf16[288,1152]{1,0:T(8,128)(2,1)} %param.22) | copy-start | bytes 1990660
  124.3 9.5 %all-to-all-start.1 = ((bf16[4,456,72]{1,2,0:T(8,128)(2,1)}), bf16[4,456,72]{1,2,0:T(8,128)(2,1)S(1)}, u32[]{:S(2)}, u32[]{:S(2)}) async-start(bf16[4,456,72]{1,2,0:T(8,128)(2,1)} %copy.73), calls=%async_computation.1 | async-start | bytes 589824 | tf_op jit(solution)/shard_map/all_to_all | solution.py:211
  133.8 4.4 copy-start.11
  135.6 9.0 %copy-start.5 = (bf16[114,1152]{1,0:T(8,128)(2,1)S(1)}, bf16[114,1152]{1,0:T(8,128)(2,1)}, u32[]{:S(2)}) copy-start(bf16[114,1152]{1,0:T(8,128)(2,1)} %param.15) | copy-start | bytes 787972
  138.2 25.4 %copy-start.21 = (f32[1152]{0:T(1024)S(1)}, f32[1152]{0:T(1024)}, u32[]{:S(2)}) copy-start(f32[1152]{0:T(1024)} %param.23) | copy-start | bytes 13828
  138.2 23.9 %all-to-all-start.2 = ((bf16[4,114,1152]{2,1,0:T(8,128)(2,1)}), bf16[4,114,1152]{2,1,0:T(8,128)(2,1)}, u32[]{:S(2)}, u32[]{:S(2)}) async-start(bf16[4,114,1152]{2,1,0:T(8,128)(2,1)} %reshape.205), calls=%async_computation.2 | async-start | bytes 2211840 | tf_op jit(solution)/shard_map/all_to_all | solution.py:139
  142.6 23.2 %all-gather.13.cloned.1.call-start = ((), (), s32[]{:S(2)}) async-start(), calls=%async_computation.13 | async-start | bytes 1382400 | tf_op jit(solution)/shard_map/all_gather | solution.py:135
  144.4 19.7 %copy-start.19 = (f32[1152]{0:T(1024)S(1)}, f32[1152]{0:T(1024)}, u32[]{:S(2)}) copy-start(f32[1152]{0:T(1024)} %param.24) | copy-start | bytes 13828
  144.4 19.7 %copy-start.22 = (f32[1152]{0:T(1024)S(1)}, f32[1152]{0:T(1024)}, u32[]{:S(2)}) copy-start(f32[1152]{0:T(1024)} %param.25) | copy-start | bytes 13828
  144.4 36.9 %all-gather.11.cloned.1.call-start = ((), (), s32[]{:S(2)}) async-start(), calls=%async_computation.12 | async-start | bytes 1382400 | tf_op jit(solution)/shard_map/all_gather | solution.py:135
  183.8 3.8 copy-start.15
  187.7 2.4 copy-start.30
  187.7 3.4 copy-start.27
  190.1 1.0 copy-start.32
  196.4 19.4 %all-to-all-start.4 = ((bf16[4,114,1152]{2,1,0:T(8,128)(2,1)}), bf16[4,114,1152]{2,1,0:T(8,128)(2,1)}, u32[]{:S(2)}, u32[]{:S(2)}) async-start(bf16[4,114,1152]{2,1,0:T(8,128)(2,1)} %reshape.207), calls=%async_computation.4 | async-start | bytes 2211840 | tf_op jit(solution)/shard_map/all_to_all | solution.py:139
  215.8 18.5 %all-to-all-start.3 = ((bf16[4,114,1152]{2,1,0:T(8,128)(2,1)}), bf16[4,114,1152]{2,1,0:T(8,128)(2,1)S(1)}, u32[]{:S(2)}, u32[]{:S(2)}) async-start(bf16[4,114,1152]{2,1,0:T(8,128)(2,1)} %reshape.206), calls=%async_computation.3 | async-start | bytes 2211840 | tf_op jit(solution)/shard_map/all_to_all | solution.py:139
  219.3 15.2 %copy-start.14 = (bf16[114,1152]{1,0:T(8,128)(2,1)S(1)}, bf16[114,1152]{1,0:T(8,128)(2,1)}, u32[]{:S(2)}) copy-start(bf16[114,1152]{1,0:T(8,128)(2,1)} %param.16) | copy-start | bytes 787972
  219.3 15.2 %copy-start.23 = (f32[1152]{0:T(1024)S(1)}, f32[1152]{0:T(1024)}, u32[]{:S(2)}) copy-start(f32[1152]{0:T(1024)} %param.29) | copy-start | bytes 13828
  219.4 34.3 %all-gather.15.cloned.1.call-start = ((), (), s32[]{:S(2)}) async-start(), calls=%async_computation.14 | async-start | bytes 1382400 | tf_op jit(solution)/shard_map/all_gather | solution.py:135
  235.6 21.6 %copy-start.6 = (f32[114,1152]{1,0:T(8,128)}, f32[114,1152]{1,0:T(8,128)S(1)}, u32[]{:S(2)}) copy-start(f32[114,1152]{1,0:T(8,128)S(1)} %get-tuple-element.100) | copy-start | bytes 1575940
  255.1 30.7 %copy-start.8 = (bf16[456,1152]{1,0:T(8,128)(2,1)}, bf16[456,1152]{1,0:T(8,128)(2,1)S(1)}, u32[]{:S(2)}) copy-start(bf16[456,1152]{1,0:T(8,128)(2,1)S(1)} %reshape.220) | copy-start | bytes 3151876
  293.1 7.2 %copy-start.17 = (f32[4,456,72]{2,1,0:T(8,128)S(1)}, f32[4,456,72]{2,1,0:T(8,128)}, u32[]{:S(2)}) copy-start(f32[4,456,72]{2,1,0:T(8,128)} %get-tuple-element.21) | copy-start | bytes 1575940
  293.2 21.8 %collective-permute-start.2 = (bf16[798,144]{1,0:T(8,128)(2,1)S(1)}, bf16[798,144]{1,0:T(8,128)(2,1)S(1)}, u32[]{:S(2)}, u32[]{:S(2)}) collective-permute-start(bf16[798,144]{1,0:T(8,128)(2,1)S(1)} %get-tuple-element.114), channel_id=1, source_target_pairs={{16,0},{20,4},{24,8},{28,12},{17,1},{21,5},{25,9},{29,13},{18,2},{... | collective-permute-start | bytes 689480 | tf_op jit(solution)/shard_map/ppermute | solution.py:262
  294.6 20.4 %collective-permute-start.3 = (bf16[798,144]{1,0:T(8,128)(2,1)S(1)}, bf16[798,144]{1,0:T(8,128)(2,1)S(1)}, u32[]{:S(2)}, u32[]{:S(2)}) collective-permute-start(bf16[798,144]{1,0:T(8,128)(2,1)S(1)} %get-tuple-element.115), channel_id=1, source_target_pairs={{0,16},{4,20},{8,24},{12,28},{1,17},{5,21},{9,25},{13,29},{2,18},{... | collective-permute-start | bytes 689480 | tf_op jit(solution)/shard_map/ppermute | solution.py:263
  322.8 24.6 %copy-start.4 = (f32[456,1152]{1,0:T(8,128)S(1)}, f32[456,1152]{1,0:T(8,128)}, u32[]{:S(2)}) copy-start(f32[456,1152]{1,0:T(8,128)} %reshape.221) | copy-start | bytes 6303748
  322.8 24.6 %copy-start.26 = (f32[456]{0:T(512)S(1)}, f32[456]{0:T(512)}, u32[]{:S(2)}) copy-start(f32[456]{0:T(512)} %copy-done.25) | copy-start | bytes 5476
  322.8 24.6 %copy-start.29 = (f32[1152]{0:T(1024)S(1)}, f32[1152]{0:T(1024)}, u32[]{:S(2)}) copy-start(f32[1152]{0:T(1024)} %param.19) | copy-start | bytes 13828
  322.8 22.2 %all-to-all-start.6 = ((bf16[16,456,72]{1,2,0:T(8,128)(2,1)}), bf16[16,456,72]{1,2,0:T(8,128)(2,1)}, u32[]{:S(2)}, u32[]{:S(2)}) async-start(bf16[16,456,72]{1,2,0:T(8,128)(2,1)} %bitcast.87), calls=%async_computation.6 | async-start | bytes 2359296 | tf_op jit(solution)/shard_map/all_to_all | solution.py:285
  327.3 134.7 %reduce-scatter.5.cloned.1.call-start = ((), (), s32[]{:S(2)}) async-start(), calls=%async_computation.10 | async-start | bytes 2322432 | tf_op jit(solution)/shard_map/reduce_scatter | solution.py:142
  346.3 1.1 copy-start.13
  350.7 184.1 %reduce-scatter.7.cloned.1.call-start = ((), (), s32[]{:S(2)}) async-start(), calls=%async_computation.15 | async-start | bytes 6635520
  351.0 4.8 copy-start.16
  351.0 4.8 copy-start.31
  355.8 3.2 copy-start.9
  355.8 3.2 copy-start.12
  404.5 56.0 %all-to-all-start.7 = ((bf16[4,114,1152]{2,1,0:T(8,128)(2,1)}), bf16[4,114,1152]{2,1,0:T(8,128)(2,1)S(1)}, u32[]{:S(2)}, u32[]{:S(2)}) async-start(bf16[4,114,1152]{2,1,0:T(8,128)(2,1)} %reshape.212), calls=%async_computation.7 | async-start | bytes 2211840 | tf_op jit(solution)/shard_map/all_to_all | solution.py:139
  411.7 49.2 %copy-start.7 = (f32[114,1152]{1,0:T(8,128)S(1)}, f32[114,1152]{1,0:T(8,128)}, u32[]{:S(2)}) copy-start(f32[114,1152]{1,0:T(8,128)} %copy-done.6) | copy-start | bytes 1575940
  536.6 1.0 copy-start.2
  537.7 8.6 %copy-start.1 = (bf16[1076,1152]{1,0:T(8,128)(2,1)S(1)}, bf16[1076,1152]{1,0:T(8,128)(2,1)}, u32[]{:S(2)}) copy-start(bf16[1076,1152]{1,0:T(8,128)(2,1)} %param.28) | copy-start | bytes 7437316
Sparse Core Ops, SparseCore 0:
  9.6 19.7 all-gather.8
  145.5 19.4 all-gather.12
  167.1 14.1 all-gather.10
  236.6 17.0 all-gather.14
  350.8 68.0 reduce-scatter.4
  422.4 112.3 reduce-scatter.6
